TPU v7x, 32 devices: a whole 2x2x4 slice. The times are simulated.
32 devices in a mesh: rep: 4 (over y, core), shard: 8 (over z, x).
Axes of the slice: x: 2, y: 2, z: 4, core: 2. Of those that a mesh axis runs over, the one named last changes fastest.
Arguments:
- tokens: bfloat16 [32768, 1024], P(('rep', 'shard')), may hold values from -6 to 6
- cotangent: bfloat16 [32768, 1024], P(('rep', 'shard')), may hold values from -6 to 6
- deal_source: int32 [4, 64], P('rep'), may hold values from 0 to 63, as said below
- deal_first: int32 [4, 64], P('rep'), may hold values from 0 to 7, as said below
- deal_length: int32 [4, 64], P('rep'), may hold values from 1 to 1024, as said below
- qkv_weight: bfloat16 [1024, 3072], P('shard'), may hold values from -0.1875 to 0.1875
- query_bias: bfloat16 [1024], P('shard'), may hold values from -3 to 3
- value_bias: bfloat16 [1024], P('shard'), may hold values from -3 to 3
- out_weight: bfloat16 [1024, 1024], P('shard'), may hold values from -0.5 to 0.5
- out_bias: bfloat16 [1024], P('shard'), may hold values from -3 to 3
- first_gain: bfloat16 [1024], P('shard'), may hold values from 0.25 to 1.75
- first_shift: bfloat16 [1024], P('shard'), may hold values from -2 to 2
- up_weight: bfloat16 [1024, 4096], P('shard'), may hold values from -0.1875 to 0.1875
- up_bias: bfloat16 [4096], P('shard'), may hold values from -3 to 3
- down_weight: bfloat16 [4096, 1024], P('shard'), may hold values from -0.09375 to 0.09375
- down_bias: bfloat16 [1024], P('shard'), may hold values from -3 to 3
- second_gain: bfloat16 [1024], P('shard'), may hold values from 0.25 to 1.75
- second_shift: bfloat16 [1024], P('shard'), may hold values from -2 to 2
Outputs:
- output: bfloat16 [32768, 1024], P(('rep', 'shard'))
- input_grad: bfloat16 [32768, 1024], P(('rep', 'shard'))
- qkv_weight_grad: float32 [1024, 3072], P('shard')
- query_bias_grad: float32 [1024], P('shard')
- value_bias_grad: float32 [1024], P('shard')
- out_weight_grad: float32 [1024, 1024], P('shard')
- out_bias_grad: float32 [1024], P('shard')
- first_gain_grad: float32 [1024], P('shard')
- first_shift_grad: float32 [1024], P('shard')
- up_weight_grad: float32 [1024, 4096], P('shard')
- up_bias_grad: float32 [4096], P('shard')
- down_weight_grad: float32 [4096, 1024], P('shard')
- down_bias_grad: float32 [1024], P('shard')
- second_gain_grad: float32 [1024], P('shard')
- second_shift_grad: float32 [1024], P('shard')
Inputs may be any that keep to these rules, and one draw needn't show every extreme that they name: `deal_source`: in each group, a permutation of the group's blocks; every sequence's blocks are consecutive and in order both in the given order and in the dealt order, and all lie on one device. `deal_first`: equal for all blocks of one sequence, and equal to the block's own local index at a sequence's first block. `deal_length`: equal for all blocks of one sequence; a sequence of n blocks has a length above (n - 1) * 128.
All inputs are finite; a program needn't handle non-finite values.
Results may differ from a plain program's by a relative error of at most 0.019.
Values may be sent and summed in bfloat16 or wider, within the bound.
No kernel may reach another device: no remote copies, remote signals or barrier semaphores. Data moves between devices by JAX's collectives and lax.ppermute only.
A program may use at most 320 MiB of HBM per device.

v0:
```python
import jax
import jax.numpy as jnp
from jax import lax
from jax.sharding import PartitionSpec as P

HDIM = 64
BLOCK = 128


NORM_EPSILON = 1e-05
heads_per_step = 4


def layer_norm(resid, gain, shift):
    row_mean = jnp.mean(resid, axis=-1, keepdims=True)
    centred = resid - row_mean
    variance = jnp.mean(centred * centred, axis=-1, keepdims=True)
    return centred * lax.rsqrt(variance + NORM_EPSILON) * gain + shift


def gelu_exact(tensor):
    return 0.5 * tensor * (1.0 + lax.erf(tensor * 0.7071067811865476))


def contract_last(left_side, right_side):
    return lax.dot_general(
        left_side, right_side, (((1,), (1,)), ((), ())), preferred_element_type=jnp.float32
    )


def head_parts(qkv_rows, group_index):
    row_count = qkv_rows.shape[0]
    feature_width = qkv_rows.shape[1] // 3
    group_span = heads_per_step * HDIM
    head_shape = (row_count, heads_per_step, HDIM)
    queries = lax.dynamic_slice_in_dim(qkv_rows, group_index * group_span, group_span, 1).reshape(
        head_shape
    )
    key_part = lax.dynamic_slice_in_dim(
        qkv_rows, feature_width + group_index * group_span, group_span, 1
    ).reshape(head_shape)
    values = lax.dynamic_slice_in_dim(
        qkv_rows, 2 * feature_width + group_index * group_span, group_span, 1
    ).reshape(head_shape)
    return (queries, key_part, values)


def masked_scores(queries, key_part, allowed):
    scores = jnp.einsum(
        "qhd,khd->hqk", queries, key_part, preferred_element_type=jnp.float32
    ) * HDIM ** (-0.5)
    return jnp.where(allowed[None], scores, -1e30)


def attend_group(qkv_rows, allowed, group_index):
    queries, key_part, values = head_parts(qkv_rows, group_index)
    scores = masked_scores(queries, key_part, allowed)
    row_max = jnp.max(scores, axis=-1, keepdims=True)
    exponent = jnp.exp(scores - row_max)
    row_total = jnp.sum(exponent, axis=-1, keepdims=True)
    rounded = (exponent / row_total).astype(jnp.bfloat16)
    mixed_heads = jnp.einsum("hqk,khd->qhd", rounded, values, preferred_element_type=jnp.float32)
    return (
        mixed_heads.reshape(qkv_rows.shape[0], -1).astype(jnp.bfloat16),
        (row_max + jnp.log(row_total))[..., 0],
    )


def attend_back(qkv_rows, mixed_grad, log_total, allowed, group_index):
    queries, key_part, values = head_parts(qkv_rows, group_index)
    row_count = qkv_rows.shape[0]
    group_span = heads_per_step * HDIM
    out_grad = lax.dynamic_slice_in_dim(
        mixed_grad, group_index * group_span, group_span, 1
    ).reshape(row_count, heads_per_step, HDIM)
    scores = masked_scores(queries, key_part, allowed)
    weights = jnp.exp(scores - log_total[..., None])
    value_grad = jnp.einsum(
        "hqk,qhd->khd", weights.astype(jnp.bfloat16), out_grad, preferred_element_type=jnp.float32
    )
    weight_grad = jnp.einsum("qhd,khd->hqk", out_grad, values, preferred_element_type=jnp.float32)
    score_grad = weights * (weight_grad - jnp.sum(weight_grad * weights, axis=-1, keepdims=True))
    score_rounded = score_grad.astype(jnp.bfloat16)
    query_grad = jnp.einsum(
        "hqk,khd->qhd", score_rounded, key_part, preferred_element_type=jnp.float32
    ) * HDIM ** (-0.5)
    key_grad = jnp.einsum(
        "hqk,qhd->khd", score_rounded, queries, preferred_element_type=jnp.float32
    ) * HDIM ** (-0.5)
    return (
        query_grad.reshape(row_count, group_span),
        key_grad.reshape(row_count, group_span),
        value_grad.reshape(row_count, group_span),
    )


def join_groups(stacked, row_count):
    return jnp.moveaxis(stacked, 0, 1).reshape(row_count, -1)


def plain_term(left_side, right_side):
    return jnp.einsum("ri,rj->ij", left_side, right_side, preferred_element_type=jnp.float32)


def local(
    tokens,
    cotangent,
    deal_source,
    deal_first,
    deal_length,
    qkv_weight,
    query_bias,
    value_bias,
    out_weight,
    out_bias,
    first_gain,
    first_shift,
    up_weight,
    up_bias,
    down_weight,
    down_bias,
    second_gain,
    second_shift,
):
    row_count, feature_width = tokens.shape
    block_rows = BLOCK
    block_count = row_count // block_rows
    place_index = lax.axis_index("shard")
    sources = deal_source[0]
    own_sources = lax.dynamic_slice_in_dim(sources, place_index * block_count, block_count)
    firsts = lax.dynamic_slice_in_dim(deal_first[0], place_index * block_count, block_count)
    lengths = lax.dynamic_slice_in_dim(deal_length[0], place_index * block_count, block_count)
    arrived = (
        lax.all_gather(tokens, "shard", axis=0, tiled=True),
        lax.all_gather(cotangent, "shard", axis=0, tiled=True),
    )
    piece_count = arrived[0].shape[0] // block_rows
    held = jnp.arange(piece_count, dtype=jnp.int32)
    selector = (own_sources[:, None] == held[None, :]).astype(jnp.bfloat16)
    moved_inputs = jnp.einsum(
        "ab,btd->atd",
        selector,
        arrived[0].reshape(piece_count, block_rows, feature_width),
        preferred_element_type=jnp.float32,
    )
    moved_grads = jnp.einsum(
        "ab,btd->atd",
        selector,
        arrived[1].reshape(piece_count, block_rows, feature_width),
        preferred_element_type=jnp.float32,
    )
    inputs = moved_inputs.reshape(row_count, feature_width).astype(jnp.bfloat16)
    grad_out = moved_grads.reshape(row_count, feature_width)
    row_first = jnp.repeat(firsts, block_rows, total_repeat_length=row_count)
    row_length = jnp.repeat(lengths, block_rows, total_repeat_length=row_count)
    position = jnp.arange(row_count, dtype=jnp.int32) - row_first * block_rows
    allowed = (row_first[:, None] == row_first[None, :]) & (position < row_length)[None, :]

    def attn_weights():
        return (
            lax.all_gather(qkv_weight, "shard", axis=0, tiled=True),
            lax.all_gather(out_weight, "shard", axis=0, tiled=True),
            lax.all_gather(query_bias, "shard", axis=0, tiled=True),
            lax.all_gather(value_bias, "shard", axis=0, tiled=True),
            lax.all_gather(out_bias, "shard", axis=0, tiled=True),
            lax.all_gather(first_gain, "shard", axis=0, tiled=True),
            lax.all_gather(first_shift, "shard", axis=0, tiled=True),
        )

    def mlp_weights():
        return (
            lax.all_gather(up_weight, "shard", axis=0, tiled=True),
            lax.all_gather(down_weight, "shard", axis=0, tiled=True),
            lax.all_gather(up_bias, "shard", axis=0, tiled=True),
            lax.all_gather(down_bias, "shard", axis=0, tiled=True),
            lax.all_gather(second_gain, "shard", axis=0, tiled=True),
            lax.all_gather(second_shift, "shard", axis=0, tiled=True),
        )

    full_qkv, full_out, bias_query, bias_value, bias_out, gain_one, shift_one = attn_weights()
    key_zeros = jnp.zeros(bias_query.shape, jnp.float32)
    qkv_bias = jnp.concatenate(
        [bias_query.astype(jnp.float32), key_zeros, bias_value.astype(jnp.float32)]
    )
    qkv_rows = (jnp.dot(inputs, full_qkv, preferred_element_type=jnp.float32) + qkv_bias).astype(
        jnp.bfloat16
    )
    group_total = feature_width // HDIM // heads_per_step
    group_ids = jnp.arange(group_total, dtype=jnp.int32)
    mixed_parts, log_totals = lax.map(
        lambda group_index: attend_group(qkv_rows, allowed, group_index), group_ids
    )
    mixed_rows = join_groups(mixed_parts, row_count)
    branch = jnp.dot(mixed_rows, full_out, preferred_element_type=jnp.float32) + bias_out.astype(
        jnp.float32
    )
    normed, first_back = jax.vjp(
        layer_norm,
        inputs.astype(jnp.float32) + branch,
        gain_one.astype(jnp.float32),
        shift_one.astype(jnp.float32),
    )
    normed_rows = normed.astype(jnp.bfloat16)
    full_up, full_down, bias_up, bias_down, gain_two, shift_two = mlp_weights()
    gate_value = jnp.dot(normed_rows, full_up, preferred_element_type=jnp.float32) + bias_up.astype(
        jnp.float32
    )
    hidden, gelu_back = jax.vjp(gelu_exact, gate_value)
    hidden_rows = hidden.astype(jnp.bfloat16)
    resid_two = (
        normed
        + jnp.dot(hidden_rows, full_down, preferred_element_type=jnp.float32)
        + bias_down.astype(jnp.float32)
    )
    result, second_back = jax.vjp(
        layer_norm, resid_two, gain_two.astype(jnp.float32), shift_two.astype(jnp.float32)
    )
    full_up, full_down, bias_up, bias_down, gain_two, shift_two = mlp_weights()
    resid_two_grad, second_gain_grad, second_shift_grad = second_back(grad_out)
    second_grad = resid_two_grad.astype(jnp.bfloat16)
    down_bias_grad = jnp.sum(second_grad.astype(jnp.float32), axis=0)
    (gate_grad_full,) = gelu_back(contract_last(second_grad, full_down))
    gate_grad = gate_grad_full.astype(jnp.bfloat16)
    up_bias_grad = jnp.sum(gate_grad.astype(jnp.float32), axis=0)
    normed_grad = resid_two_grad + contract_last(gate_grad, full_up)
    resid_one_grad, first_gain_grad, first_shift_grad = first_back(normed_grad)
    branch_grad = resid_one_grad.astype(jnp.bfloat16)
    out_bias_grad = jnp.sum(branch_grad.astype(jnp.float32), axis=0)
    full_qkv, full_out, bias_query, bias_value, bias_out, gain_one, shift_one = attn_weights()
    mixed_grad = contract_last(branch_grad, full_out).astype(jnp.bfloat16)
    query_parts, key_parts, value_parts = lax.map(
        lambda item: attend_back(qkv_rows, mixed_grad, item[1], allowed, item[0]),
        (group_ids, log_totals),
    )
    qkv_grad = jnp.concatenate(
        [
            join_groups(query_parts, row_count),
            join_groups(key_parts, row_count),
            join_groups(value_parts, row_count),
        ],
        axis=1,
    ).astype(jnp.bfloat16)
    query_bias_grad = jnp.sum(qkv_grad[:, :feature_width].astype(jnp.float32), axis=0)
    value_bias_grad = jnp.sum(qkv_grad[:, 2 * feature_width :].astype(jnp.float32), axis=0)
    input_grad = resid_one_grad + contract_last(qkv_grad, full_qkv)
    full_qkv_grad = jnp.einsum("ri,rj->ij", inputs, qkv_grad, preferred_element_type=jnp.float32)
    full_out_grad = jnp.einsum(
        "ri,rj->ij", mixed_rows, branch_grad, preferred_element_type=jnp.float32
    )
    up_part = lax.psum_scatter(
        plain_term(normed_rows, gate_grad).astype(jnp.bfloat16),
        "shard",
        scatter_dimension=0,
        tiled=True,
    )
    down_part = lax.psum_scatter(
        plain_term(hidden_rows, second_grad).astype(jnp.bfloat16),
        "shard",
        scatter_dimension=0,
        tiled=True,
    )
    owned = (
        lax.psum_scatter(
            full_qkv_grad.astype(jnp.bfloat16), "shard", scatter_dimension=0, tiled=True
        ).astype(jnp.float32),
        lax.psum_scatter(
            full_out_grad.astype(jnp.bfloat16), "shard", scatter_dimension=0, tiled=True
        ).astype(jnp.float32),
        lax.psum_scatter(
            query_bias_grad.astype(jnp.bfloat16), "shard", scatter_dimension=0, tiled=True
        ).astype(jnp.float32),
        lax.psum_scatter(
            value_bias_grad.astype(jnp.bfloat16), "shard", scatter_dimension=0, tiled=True
        ).astype(jnp.float32),
        lax.psum_scatter(
            out_bias_grad.astype(jnp.bfloat16), "shard", scatter_dimension=0, tiled=True
        ).astype(jnp.float32),
        lax.psum_scatter(
            first_gain_grad.astype(jnp.bfloat16), "shard", scatter_dimension=0, tiled=True
        ).astype(jnp.float32),
        lax.psum_scatter(
            first_shift_grad.astype(jnp.bfloat16), "shard", scatter_dimension=0, tiled=True
        ).astype(jnp.float32),
        lax.psum_scatter(
            up_bias_grad.astype(jnp.bfloat16), "shard", scatter_dimension=0, tiled=True
        ).astype(jnp.float32),
        lax.psum_scatter(
            down_bias_grad.astype(jnp.bfloat16), "shard", scatter_dimension=0, tiled=True
        ).astype(jnp.float32),
        lax.psum_scatter(
            second_gain_grad.astype(jnp.bfloat16), "shard", scatter_dimension=0, tiled=True
        ).astype(jnp.float32),
        lax.psum_scatter(
            second_shift_grad.astype(jnp.bfloat16), "shard", scatter_dimension=0, tiled=True
        ).astype(jnp.float32),
    )
    summed = (
        lax.psum(up_part, "rep").astype(jnp.float32),
        lax.psum(down_part, "rep").astype(jnp.float32),
        lax.psum(owned[0].astype(jnp.bfloat16), "rep").astype(jnp.float32),
        lax.psum(owned[1].astype(jnp.bfloat16), "rep").astype(jnp.float32),
        lax.psum(owned[2].astype(jnp.bfloat16), "rep").astype(jnp.float32),
        lax.psum(owned[3].astype(jnp.bfloat16), "rep").astype(jnp.float32),
        lax.psum(owned[4].astype(jnp.bfloat16), "rep").astype(jnp.float32),
        lax.psum(owned[5].astype(jnp.bfloat16), "rep").astype(jnp.float32),
        lax.psum(owned[6].astype(jnp.bfloat16), "rep").astype(jnp.float32),
        lax.psum(owned[7].astype(jnp.bfloat16), "rep").astype(jnp.float32),
        lax.psum(owned[8].astype(jnp.bfloat16), "rep").astype(jnp.float32),
        lax.psum(owned[9].astype(jnp.bfloat16), "rep").astype(jnp.float32),
        lax.psum(owned[10].astype(jnp.bfloat16), "rep").astype(jnp.float32),
    )
    result_rows = result.astype(jnp.bfloat16)
    back_rows = input_grad.astype(jnp.bfloat16)
    wanted = place_index * block_count + jnp.arange(block_count, dtype=jnp.int32)
    arrived = (
        lax.all_gather(result_rows, "shard", axis=0, tiled=True),
        lax.all_gather(back_rows, "shard", axis=0, tiled=True),
    )
    piece_count = arrived[0].shape[0] // block_rows
    held = sources
    selector = (wanted[:, None] == held[None, :]).astype(jnp.bfloat16)
    moved_out = jnp.einsum(
        "ab,btd->atd",
        selector,
        arrived[0].reshape(piece_count, block_rows, feature_width),
        preferred_element_type=jnp.float32,
    )
    moved_back = jnp.einsum(
        "ab,btd->atd",
        selector,
        arrived[1].reshape(piece_count, block_rows, feature_width),
        preferred_element_type=jnp.float32,
    )
    output = moved_out.reshape(row_count, feature_width).astype(jnp.bfloat16)
    input_rows = moved_back.reshape(row_count, feature_width).astype(jnp.bfloat16)
    return (
        output,
        input_rows,
        summed[2],
        summed[4],
        summed[5],
        summed[3],
        summed[6],
        summed[7],
        summed[8],
        summed[0],
        summed[9],
        summed[1],
        summed[10],
        summed[11],
        summed[12],
    )


def solution(mesh):
    return jax.shard_map(
        local,
        mesh=mesh,
        in_specs=(
            P(("rep", "shard"), None),
            P(("rep", "shard"), None),
            P("rep", None),
            P("rep", None),
            P("rep", None),
            P("shard", None),
            P("shard"),
            P("shard"),
            P("shard", None),
            P("shard"),
            P("shard"),
            P("shard"),
            P("shard", None),
            P("shard"),
            P("shard", None),
            P("shard"),
            P("shard"),
            P("shard"),
        ),
        out_specs=(
            P(("rep", "shard"), None),
            P(("rep", "shard"), None),
            P("shard", None),
            P("shard"),
            P("shard"),
            P("shard", None),
            P("shard"),
            P("shard"),
            P("shard"),
            P("shard", None),
            P("shard"),
            P("shard", None),
            P("shard"),
            P("shard"),
            P("shard"),
        ),
        check_vma=False,
    )
```

profile of v0, /device:TPU:0, one launch (start us, length us, event | category | flops | bytes accessed | tf_op | source)
XLA Modules:
  0.0 2177.5 jit_solution(11480984906767941914)
XLA Ops:
  12.8 22.7 %all-gather = bf16[8,1,128]{2,1,0:T(2,128)(2,1)S(1)} all-gather(bf16[1,1,128]{2,1,0:T(2,128)(2,1)S(1)} %bitcast.321), channel_id=1, replica_groups=mesh['rep'=4,'shard'=8] {'shard'}, dimensions={0}, use_global_device_ids=true | all-gather | bytes 2304 | tf_op jit(solution)/shard_map/all_gather | solution.py:163
  52.5 19.2 all-gather.2
  109.0 27.4 %all-gather.5 = bf16[8,1,512]{2,1,0:T(2,128)(2,1)S(1)} all-gather(bf16[1,1,512]{2,1,0:T(2,128)(2,1)S(1)} %reshape.355), channel_id=1, replica_groups=mesh['rep'=4,'shard'=8] {'shard'}, dimensions={0}, use_global_device_ids=true | all-gather | bytes 9216 | tf_op jit(solution)/shard_map/all_gather | solution.py:174
  156.8 25.3 %all-gather.7 = bf16[8,1,128]{2,1,0:T(2,128)(2,1)S(1)} all-gather(bf16[1,1,128]{2,1,0:T(2,128)(2,1)S(1)} %bitcast.327), channel_id=1, replica_groups=mesh['rep'=4,'shard'=8] {'shard'}, dimensions={0}, use_global_device_ids=true | all-gather | bytes 2304 | tf_op jit(solution)/shard_map/all_gather | solution.py:176
  182.7 22.0 %all-gather.8 = bf16[8,1,128]{2,1,0:T(2,128)(2,1)S(1)} all-gather(bf16[1,1,128]{2,1,0:T(2,128)(2,1)S(1)} %bitcast.328), channel_id=1, replica_groups=mesh['rep'=4,'shard'=8] {'shard'}, dimensions={0}, use_global_device_ids=true | all-gather | bytes 2304 | tf_op jit(solution)/shard_map/all_gather | solution.py:177
  220.5 20.3 all-gather.18.cloned.1.call-done
  240.8 23.8 %fusion.19 = bf16[8,128,1024]{2,0,1:T(8,128)(2,1)S(1)} fusion(bf16[64,128,1024]{2,1,0:T(8,128)(2,1)} %bitcast.286, s32[8]{0:T(128)S(1)} %fusion.47), kind=kOutput, calls=%fused_computation.67 | convolution fusion | flops 135266816 | bytes 18874400 | tf_op jit(solution)/shard_map/ab,btd->atd/dot_general | solution.py:140
  268.8 71.2 %all-gather.20.cloned.1.call-done = bf16[1024,3072]{1,0:T(8,128)(2,1)} async-done(((bf16[128,3072]{1,0:T(8,128)(2,1)}), bf16[1024,3072]{1,0:T(8,128)(2,1)}) %all-gather.20.cloned.1.call-update) | async-done | bytes 6291472 | tf_op jit(solution)/shard_map/all_gather | solution.py:161
  359.9 66.4 %while.34 = (s32[]{:T(128)}, bf16[4,1024,256]{1,2,0:T(8,128)(2,1)}, f32[4,4,1024]{2,1,0:T(4,128)S(1)}, s32[4]{0:T(128)S(1)}, bf16[1024,3072]{0,1:T(8,128)(2,1)},...) while((s32[]{:T(128)}, bf16[4,1024,256]{1,2,0:T(8,128)(2,1)}, ...), condition=%wide.region_3.5_spmd.clone, body=%wide.region_0.4_spmd.clone.sunk | while | flops 1126428672 | bytes 60954420 | solution.py:190
  433.8 80.6 %all-gather.24.cloned.1.call-done = bf16[1024,4096]{1,0:T(8,128)(2,1)} async-done(((bf16[128,4096]{1,0:T(8,128)(2,1)}), bf16[1024,4096]{1,0:T(8,128)(2,1)}) %all-gather.24.cloned.1.call-update) | async-done | bytes 8388624 | tf_op jit(solution)/shard_map/all_gather | solution.py:172
  514.5 20.2 multiply_convert_fusion.1
  534.7 104.5 %all-gather.26.cloned.1.call-done = bf16[4096,1024]{1,0:T(8,128)(2,1)} async-done(((bf16[512,1024]{1,0:T(8,128)(2,1)}), bf16[4096,1024]{1,0:T(8,128)(2,1)}) %all-gather.26.cloned.1.call-update) | async-done | bytes 8388624 | tf_op jit(solution)/shard_map/all_gather | solution.py:173
  657.0 209.6 %all-gather.30.cloned.1.call-done = bf16[8192,1024]{1,0:T(8,128)(2,1)} async-done(((bf16[1024,1024]{1,0:T(8,128)(2,1)}), bf16[8192,1024]{1,0:T(8,128)(2,1)}) %all-gather.30.cloned.1.call-update) | async-done | bytes 16777232 | tf_op jit(solution)/shard_map/all_gather | solution.py:135
  866.6 26.1 %fusion.64 = (bf16[1024]{0:T(1024)(128)(2,1)}, f32[8,128,1024]{2,0,1:T(8,128)}) fusion(bf16[64,128,1024]{2,1,0:T(8,128)(2,1)} %bitcast.285, s32[8]{0:T(128)S(1)} %copy-done.37), kind=kOutput, calls=%fused_computation.127 | convolution fusion | flops 135265792 | bytes 20973600 | tf_op jit(solution)/shard_map/ab,btd->atd/dot_general | solution.py:146
  908.1 22.1 %fusion.56 = (bf16[4096]{0:T(1024)(128)(2,1)}, bf16[1024,4096]{1,0:T(8,128)(2,1)}) fusion(f32[1024,4096]{1,0:T(8,128)} %get-tuple-element.432, f32[4096]{0:T(1024)S(1)} %bitcast.306, bf16[1024,1024]{0,1:T(8,128)(2,1)S(1)} %get-tuple-element.391, bf16[4096,1024]{1,0:T(8,128)(2,1)} %all-gather.26.cloned.1.call-done), kind=kOutput, calls=%fused_computation.119 | convolution fusion | flops 8652845056 | bytes 35676160 | tf_op jit(solution)/shard_map/dot_general | solution.py:26
  958.7 202.2 %while.35 = (s32[]{:T(128)}, bf16[4,1024,256]{1,2,0:T(8,128)(2,1)}, bf16[4,1024,256]{1,2,0:T(8,128)(2,1)}, bf16[4,1024,256]{1,2,0:T(8,128)(2,1)}, s32[4]{0:T(128...) while((s32[]{:T(128)}, bf16[4,1024,256]{1,2,0:T(8,128)(2,1)}, ...), condition=%wide.region_14.16_spmd.clone, body=%wide.region_12.15_spmd.clone.sunk | while | flops 2725244928 | bytes 225532384 | solution.py:231
  1206.7 83.5 %reduce-scatter.5.cloned.1.call-done = bf16[128,3072]{1,0:T(8,128)(2,1)} async-done(((bf16[1024,3072]{1,0:T(8,128)(2,1)}), bf16[128,3072]{1,0:T(8,128)(2,1)}) %reduce-scatter.5.cloned.1.call-update) | async-done | bytes 786448 | tf_op jit(solution)/shard_map/reduce_scatter | solution.py:263
  1290.2 150.4 %reduce-scatter.9.cloned.1.call-done = bf16[128,4096]{1,0:T(8,128)(2,1)} async-done(((bf16[1024,4096]{1,0:T(8,128)(2,1)}), bf16[128,4096]{1,0:T(8,128)(2,1)}) %reduce-scatter.9.cloned.1.call-update) | async-done | bytes 1048592 | tf_op jit(solution)/shard_map/reduce_scatter | solution.py:250
  1440.6 150.1 %reduce-scatter.11.cloned.1.call-done = bf16[512,1024]{1,0:T(8,128)(2,1)} async-done(((bf16[4096,1024]{1,0:T(8,128)(2,1)}), bf16[512,1024]{1,0:T(8,128)(2,1)}) %reduce-scatter.11.cloned.1.call-update) | async-done | bytes 1048592 | tf_op jit(solution)/shard_map/reduce_scatter | solution.py:256
  1608.0 35.2 %all-reduce.9 = (bf16[1024]{0:T(1024)(128)(2,1)S(1)}, bf16[1024]{0:T(1024)(128)(2,1)S(1)}, bf16[1024]{0:T(1024)(128)(2,1)S(1)}, bf16[1024]{0:T(1024)(128)(2,1)S(...) all-reduce(bf16[1024]{0:T(1024)(128)(2,1)S(1)} %bitcast.312, ...), channel_id=3, replica_groups=mesh['rep'=4,'shard'=8] {'shard'}, use_global_device_ids=true, to_apply=%region_18.20.clone | all-reduce | flops 12288 | bytes 49152
  1669.0 221.6 %all-gather.32.cloned.1.call-done = bf16[8192,1024]{0,1:T(8,128)(2,1)} async-done(((bf16[1024,1024]{0,1:T(8,128)(2,1)}), bf16[8192,1024]{0,1:T(8,128)(2,1)}) %all-gather.32.cloned.1.call-update) | async-done | bytes 16777232 | tf_op jit(solution)/shard_map/all_gather | solution.py:317
  1906.4 26.0 %copy.79 = bf16[64,128,1024]{2,0,1:T(8,128)(2,1)} copy(bf16[64,128,1024]{1,0,2:T(8,128)(2,1)} %bitcast.273) | data formatting | bytes 33554432 | tf_op jit(solution)/shard_map/reshape | solution.py:331
  1943.1 175.7 %all-gather.28.cloned.1.call-done = bf16[8192,1024]{0,1:T(8,128)(2,1)} async-done(((bf16[1024,1024]{0,1:T(8,128)(2,1)}), bf16[8192,1024]{0,1:T(8,128)(2,1)}) %all-gather.28.cloned.1.call-update) | async-done | bytes 16777232 | tf_op jit(solution)/shard_map/all_gather | solution.py:316
  2134.0 26.0 %copy.71 = bf16[64,128,1024]{2,0,1:T(8,128)(2,1)} copy(bf16[64,128,1024]{1,0,2:T(8,128)(2,1)} %bitcast.274) | data formatting | bytes 33554432 | tf_op jit(solution)/shard_map/reshape | solution.py:325
  (361 shorter events, 591.6 us)
Async XLA Ops:
  7.3 101.7 %copy-start.40 = (bf16[512]{0:T(512)(128)(2,1)S(1)}, bf16[512]{0:T(512)(128)(2,1)}, u32[]{:S(2)}) copy-start(bf16[512]{0:T(512)(128)(2,1)} %param.41) | copy-start | bytes 3076
  7.3 129.7 %copy-start.48 = (bf16[128]{0:T(256)(128)(2,1)S(1)}, bf16[128]{0:T(256)(128)(2,1)}, u32[]{:S(2)}) copy-start(bf16[128]{0:T(256)(128)(2,1)} %param.43) | copy-start | bytes 772
  7.3 149.5 %copy-start.49 = (bf16[128]{0:T(256)(128)(2,1)S(1)}, bf16[128]{0:T(256)(128)(2,1)}, u32[]{:S(2)}) copy-start(bf16[128]{0:T(256)(128)(2,1)} %param.44) | copy-start | bytes 772
  7.3 175.4 %copy-start.50 = (bf16[128]{0:T(256)(128)(2,1)S(1)}, bf16[128]{0:T(256)(128)(2,1)}, u32[]{:S(2)}) copy-start(bf16[128]{0:T(256)(128)(2,1)} %param.45) | copy-start | bytes 772
  7.3 233.5 %all-gather.18.cloned.1.call-start = ((), (), s32[]{:S(2)}) async-start(), calls=%async_computation.4 | async-start | bytes 18874368 | tf_op jit(solution)/shard_map/all_gather | solution.py:134
  8.0 331.9 %all-gather.20.cloned.1.call-start = ((), (), s32[]{:S(2)}) async-start(), calls=%async_computation.5 | async-start | bytes 7077888 | tf_op jit(solution)/shard_map/all_gather | solution.py:161
  8.8 417.5 %all-gather.22.cloned.1.call-start = ((), (), s32[]{:S(2)}) async-start(), calls=%async_computation.6 | async-start | bytes 2359296 | tf_op jit(solution)/shard_map/all_gather | solution.py:162
  9.5 504.9 %all-gather.24.cloned.1.call-start = ((), (), s32[]{:S(2)}) async-start(), calls=%async_computation.7 | async-start | bytes 9437184 | tf_op jit(solution)/shard_map/all_gather | solution.py:172
  10.1 629.0 %all-gather.26.cloned.1.call-start = ((), (), s32[]{:S(2)}) async-start(), calls=%async_computation.8 | async-start | bytes 9437184 | tf_op jit(solution)/shard_map/all_gather | solution.py:173
  10.7 855.9 %all-gather.30.cloned.1.call-start = ((), (), s32[]{:S(2)}) async-start(), calls=%async_computation.10 | async-start | bytes 18874368 | tf_op jit(solution)/shard_map/all_gather | solution.py:135
  11.3 1195.4 %reduce-scatter.7.cloned.1.call-start = ((), (), s32[]{:S(2)}) async-start(), calls=%async_computation.13 | async-start | bytes 2359296 | tf_op jit(solution)/shard_map/reduce_scatter | solution.py:266
  12.8 251.8 %copy-start.36 = (s32[8]{0:T(128)}, s32[8]{0:T(128)S(1)}, u32[]{:S(2)}) copy-start(s32[8]{0:T(128)S(1)} %fusion.47) | copy-start | bytes 100
  431.4 512.2 %copy-start.14 = (f32[1024]{0:T(1024)}, f32[1024]{0:T(1024)S(1)}, u32[]{:S(2)}) copy-start(f32[1024]{0:T(1024)S(1)} %broadcast_multiply_fusion.1) | copy-start | bytes 12292
  433.8 509.8 %copy-start.19 = (f32[1024]{0:T(1024)}, f32[1024]{0:T(1024)S(1)}, u32[]{:S(2)}) copy-start(f32[1024]{0:T(1024)S(1)} %fusion.39) | copy-start | bytes 12292
  514.5 124.7 %copy-start.32 = (f32[8,1,128]{2,1,0:T(1,128)S(1)}, f32[8,1,128]{2,1,0:T(1,128)}, u32[]{:S(2)}) copy-start(f32[8,1,128]{2,1,0:T(1,128)} %convert_element_type.262) | copy-start | bytes 12292
  654.4 212.2 %copy-start.37 = (s32[8]{0:T(128)S(1)}, s32[8]{0:T(128)}, u32[]{:S(2)}) copy-start(s32[8]{0:T(128)} %copy-done.36) | copy-start | bytes 100
  953.0 337.2 %reduce-scatter.5.cloned.1.call-start = ((), (), s32[]{:S(2)}) async-start(), calls=%async_computation.12 | async-start | bytes 7077888 | tf_op jit(solution)/shard_map/reduce_scatter | solution.py:263
  1173.8 266.8 %reduce-scatter.9.cloned.1.call-start = ((), (), s32[]{:S(2)}) async-start(), calls=%async_computation.14 | async-start | bytes 9437184 | tf_op jit(solution)/shard_map/reduce_scatter | solution.py:250
  1189.9 400.8 %reduce-scatter.11.cloned.1.call-start = ((), (), s32[]{:S(2)}) async-start(), calls=%async_computation.15 | async-start | bytes 9437184 | tf_op jit(solution)/shard_map/reduce_scatter | solution.py:256
  1206.6 384.2 %copy-start.10 = (bf16[4,1024,256]{1,2,0:T(8,128)(2,1)S(1)}, bf16[4,1024,256]{1,2,0:T(8,128)(2,1)}, u32[]{:S(2)}) copy-start(bf16[4,1024,256]{1,2,0:T(8,128)(2,1)} %get-tuple-element.235) | copy-start | bytes 6291460
  1206.6 384.2 %copy-start.22 = (f32[1024]{0:T(1024)S(1)}, f32[1024]{0:T(1024)}, u32[]{:S(2)}) copy-start(f32[1024]{0:T(1024)} %copy-done.21) | copy-start | bytes 12292
  1206.6 454.6 %all-reduce.14.cloned.1.call-start = ((), (), s32[]{:S(2)}) async-start(), calls=%async_computation.16 | async-start | bytes 6291456 | tf_op jit(solution)/shard_map/psum | solution.py:300
  1590.7 299.9 %all-gather.32.cloned.1.call-start = ((), (), s32[]{:S(2)}) async-start(), calls=%async_computation.11 | async-start | bytes 18874368 | tf_op jit(solution)/shard_map/all_gather | solution.py:317
  1602.9 516.0 %all-gather.28.cloned.1.call-start = ((), (), s32[]{:S(2)}) async-start(), calls=%async_computation.9 | async-start | bytes 18874368 | tf_op jit(solution)/shard_map/all_gather | solution.py:316
  (62 other events, 1174.0 us)
Sparse Core Ops, SparseCore 0:
  10.2 230.5 all-gather.17
  243.0 96.8 all-gather.19
  342.1 47.3 all-gather.21
  391.4 122.9 all-gather.23
  516.4 122.6 all-gather.25
  641.1 225.4 all-gather.29
  953.1 66.4 reduce-scatter.6
  1173.9 116.1 reduce-scatter.4
  1293.8 146.7 reduce-scatter.8
  1444.1 146.5 reduce-scatter.10
  1593.3 67.8 all-reduce.13
  1663.3 227.3 all-gather.31
  1893.4 225.4 all-gather.27
where the time goes:
time: 2190 us; the launch traced here: 2180 us
  waiting for transfers between devices  1280 us (58%)
  matrix products  387 us (18%)
  blocking collectives  230 us (11%)
  local copies, waits for them, and re-layouts  158 us (7%)
  other arithmetic  101 us (5%)
    all_gather x1, waiting for transfers between devices, local(): lax.all_gather(back_rows, 'shard', axis=0, tiled=True)  222 us
    all_gather x1, waiting for transfers between devices, local(): lax.all_gather(cotangent, 'shard', axis=0, tiled=True)  210 us
    all_gather x1, waiting for transfers between devices, local(): lax.all_gather(result_rows, 'shard', axis=0, tiled=True)  176 us
    reduce_scatter x1, waiting for transfers between devices, local(): lax.psum_scatter(plain_term(normed_rows, gate_grad).astype(jnp.bfloat16),...  150 us
    reduce_scatter x1, waiting for transfers between devices, local(): lax.psum_scatter(plain_term(hidden_rows, second_grad).astype(jnp.bfloat16...  150 us
    all_gather x1, waiting for transfers between devices, mlp_weights(): lax.all_gather(down_weight, 'shard', axis=0, tiled=True)  104 us
    reduce_scatter x1, waiting for transfers between devices, local(): lax.psum_scatter(full_qkv_grad.astype(jnp.bfloat16), 'shard', scatter_dim...  83.5 us
    all_gather x1, waiting for transfers between devices, mlp_weights(): lax.all_gather(up_weight, 'shard', axis=0, tiled=True)  80.6 us
  transfers between devices with their start and end apart: 13, of which 11 were waited for; matrix products, arithmetic and copies ran while one was open for 23% of the time, Pallas kernels for 0%

commit v1 on v0

v1 whole, which is shorter than its diff:
```python
import functools

import jax
import jax.numpy as jnp
from jax import lax
from jax.experimental import pallas as pl
from jax.experimental.pallas import tpu as pltpu
from jax.sharding import PartitionSpec as P

HDIM = 64
BLOCK = 128
PAIR = 2 * HDIM
NORM_EPSILON = 1e-05
NEGATIVE = -1e30


def layer_norm(resid, gain, shift):
    row_mean = jnp.mean(resid, axis=-1, keepdims=True)
    centred = resid - row_mean
    variance = jnp.mean(centred * centred, axis=-1, keepdims=True)
    return centred * lax.rsqrt(variance + NORM_EPSILON) * gain + shift


def gelu_exact(tensor):
    return 0.5 * tensor * (1.0 + lax.erf(tensor * 0.7071067811865476))


def contract_last(left_side, right_side):
    return lax.dot_general(
        left_side, right_side, (((1,), (1,)), ((), ())), preferred_element_type=jnp.float32
    )


def contract_rows(left_side, right_side):
    return lax.dot_general(
        left_side, right_side, (((0,), (0,)), ((), ())), preferred_element_type=jnp.float32
    )


def matmul(left_side, right_side):
    return jnp.dot(left_side, right_side, preferred_element_type=jnp.float32)


def sizes_of(block_count):
    sizes = [1]
    while sizes[-1] < block_count:
        sizes.append(min(2 * sizes[-1], block_count))
    return sizes


def by_size(length, block_count, body):
    sizes = sizes_of(block_count)
    for index, size in enumerate(sizes):
        fits = length <= size * BLOCK
        if index > 0:
            fits = fits & (length > sizes[index - 1] * BLOCK)
        pl.when(fits)(functools.partial(body, size * BLOCK))


def stack_heads(rows):
    lane = lax.broadcasted_iota(jnp.int32, rows.shape, 1)
    zero = jnp.zeros_like(rows)
    return jnp.concatenate(
        [jnp.where(lane < HDIM, rows, zero), jnp.where(lane >= HDIM, rows, zero)], axis=0
    )


def forward_kernel(info, qkv, out, *, halo, block_count):
    def one_block(index, carry):
        first = info[0, halo + index]
        length = info[1, halo + index]
        row = pl.multiple_of((halo + index) * BLOCK, BLOCK)

        def body(size):
            start = pl.multiple_of(first * BLOCK, BLOCK)
            queries = stack_heads(qkv[pl.ds(row, BLOCK), :PAIR] * jnp.bfloat16(HDIM ** (-0.5)))
            keys = qkv[pl.ds(start, size), PAIR : 2 * PAIR]
            values = qkv[pl.ds(start, size), 2 * PAIR :]
            scores = contract_last(queries, keys)
            column = lax.broadcasted_iota(jnp.int32, scores.shape, 1)
            scores = jnp.where(column < length, scores, NEGATIVE)
            exponent = jnp.exp(scores - jnp.max(scores, axis=1, keepdims=True))
            total = jnp.sum(exponent, axis=1, keepdims=True)
            mixed = matmul(exponent.astype(jnp.bfloat16), values) / total
            lane = lax.broadcasted_iota(jnp.int32, (BLOCK, PAIR), 1)
            out[pl.ds(pl.multiple_of(index * BLOCK, BLOCK), BLOCK), :] = jnp.where(
                lane < HDIM, mixed[:BLOCK], mixed[BLOCK:]
            ).astype(jnp.bfloat16)

        by_size(length, block_count, body)
        return carry

    lax.fori_loop(0, block_count, one_block, 0)


def backward_kernel(info, qkv, mixed_grad, out, key_turned, key_sum, value_sum, *, halo, block_count):
    key_turned[...] = qkv[:, PAIR : 2 * PAIR].astype(jnp.float32).T.astype(jnp.bfloat16)
    key_sum[...] = jnp.zeros_like(key_sum)
    value_sum[...] = jnp.zeros_like(value_sum)

    def one_block(index, carry):
        first = info[0, index]
        length = info[1, index]
        row = pl.multiple_of(index * BLOCK, BLOCK)

        def body(size):
            start = pl.multiple_of(first * BLOCK, BLOCK)
            queries = stack_heads(qkv[pl.ds(row, BLOCK), :PAIR] * jnp.bfloat16(HDIM ** (-0.5)))
            grads = stack_heads(mixed_grad[pl.ds(row, BLOCK), :])
            keys = qkv[pl.ds(start, size), PAIR : 2 * PAIR]
            values = qkv[pl.ds(start, size), 2 * PAIR :]
            scores = contract_last(keys, queries)
            place = lax.broadcasted_iota(jnp.int32, scores.shape, 0)
            scores = jnp.where(place < length, scores, NEGATIVE)
            exponent = jnp.exp(scores - jnp.max(scores, axis=0, keepdims=True))
            weights = exponent * (1.0 / jnp.sum(exponent, axis=0, keepdims=True))
            value_sum[pl.ds(start, size), :] += matmul(weights.astype(jnp.bfloat16), grads)
            weight_grad = contract_last(values, grads)
            shared = jnp.sum(weights * weight_grad, axis=0, keepdims=True)
            score_grad = (weights * (weight_grad - shared)).astype(jnp.bfloat16)
            key_sum[pl.ds(start, size), :] += matmul(score_grad, queries)

            @pl.when((index >= halo) & (index < halo + block_count))
            def _():
                turned = matmul(key_turned[:, pl.ds(start, size)], score_grad)
                lane = lax.broadcasted_iota(jnp.int32, (PAIR, BLOCK), 0)
                query_grad = jnp.where(lane < HDIM, turned[:, :BLOCK], turned[:, BLOCK:]).T
                own = pl.multiple_of((index - halo) * BLOCK, BLOCK)
                out[pl.ds(own, BLOCK), :PAIR] = (query_grad * HDIM ** (-0.5)).astype(jnp.bfloat16)

        by_size(length, block_count, body)
        return carry

    lax.fori_loop(info[2, 0], info[2, 1], one_block, 0)
    own_rows = block_count * BLOCK
    out[:, PAIR : 2 * PAIR] = key_sum[halo * BLOCK : halo * BLOCK + own_rows, :].astype(jnp.bfloat16)
    out[:, 2 * PAIR :] = value_sum[halo * BLOCK : halo * BLOCK + own_rows, :].astype(jnp.bfloat16)


def attend(info, qkv_window, halo, block_count):
    window_rows, width = qkv_window.shape
    pairs = width // (3 * PAIR)
    own_rows = block_count * BLOCK
    return pl.pallas_call(
        functools.partial(forward_kernel, halo=halo, block_count=block_count),
        grid_spec=pltpu.PrefetchScalarGridSpec(
            num_scalar_prefetch=1,
            grid=(pairs,),
            in_specs=[pl.BlockSpec((window_rows, 3 * PAIR), lambda pair, info: (0, pair))],
            out_specs=pl.BlockSpec((own_rows, PAIR), lambda pair, info: (0, pair)),
        ),
        out_shape=jax.ShapeDtypeStruct((own_rows, pairs * PAIR), jnp.bfloat16),
        name="attend",
    )(info, qkv_window)


def attend_back(info, qkv_window, grad_window, halo, block_count):
    window_rows, width = qkv_window.shape
    pairs = width // (3 * PAIR)
    own_rows = block_count * BLOCK
    return pl.pallas_call(
        functools.partial(backward_kernel, halo=halo, block_count=block_count),
        grid_spec=pltpu.PrefetchScalarGridSpec(
            num_scalar_prefetch=1,
            grid=(pairs,),
            in_specs=[
                pl.BlockSpec((window_rows, 3 * PAIR), lambda pair, info: (0, pair)),
                pl.BlockSpec((window_rows, PAIR), lambda pair, info: (0, pair)),
            ],
            out_specs=pl.BlockSpec((own_rows, 3 * PAIR), lambda pair, info: (0, pair)),
            scratch_shapes=[
                pltpu.VMEM((PAIR, window_rows), jnp.bfloat16),
                pltpu.VMEM((window_rows, PAIR), jnp.float32),
                pltpu.VMEM((window_rows, PAIR), jnp.float32),
            ],
        ),
        out_shape=jax.ShapeDtypeStruct((own_rows, width), jnp.bfloat16),
        name="attend_back",
    )(info, qkv_window, grad_window)


def window_info(sources, firsts, lengths, shard, block_count, halo):
    slot_count = sources.shape[0]
    slots = jnp.arange(slot_count, dtype=jnp.int32)
    first_slot = slots // block_count * block_count + firsts
    first_given = jnp.sum(
        jnp.where(first_slot[:, None] == slots[None, :], sources[None, :], 0), axis=1
    )
    window = 2 * halo + block_count
    low = shard * block_count - halo
    given = low + jnp.arange(window, dtype=jnp.int32)
    here = sources[None, :] == given[:, None]
    start = jnp.sum(jnp.where(here, first_given[None, :], 0), axis=1) - low
    length = jnp.sum(jnp.where(here, lengths[None, :], 0), axis=1)
    last = start + (length + BLOCK - 1) // BLOCK
    begin = jnp.minimum(start[halo], halo)
    end = jnp.maximum(last[halo + block_count - 1], halo + block_count)
    bounds = jnp.where(jnp.arange(window) == 0, begin, jnp.where(jnp.arange(window) == 1, end, 0))
    return jnp.stack([start, length, bounds]).astype(jnp.int32)


def with_halo(rows, halo_rows, shard_count):
    up = [(index, index + 1) for index in range(shard_count - 1)]
    down = [(index + 1, index) for index in range(shard_count - 1)]
    left = lax.ppermute(rows[rows.shape[0] - halo_rows :], "shard", up)
    right = lax.ppermute(rows[:halo_rows], "shard", down)
    return jnp.concatenate([left, rows, right], axis=0)


def pack_small(parts, row_count):
    flat = jnp.concatenate(parts)
    width = -(-flat.shape[0] // (128 * row_count)) * 128
    return jnp.pad(flat, (0, row_count * width - flat.shape[0])).reshape(row_count, width)


def make_local(rep_count, shard_count):
    core_pairs = [(index, index ^ 1) for index in range(rep_count)]
    same_core = [list(range(core, rep_count, 2)) for core in range(2)]

    def sum_owned(summand, core):
        half = summand.shape[1] // 2
        own = lax.dynamic_slice_in_dim(summand, core * half, half, 1)
        other = lax.dynamic_slice_in_dim(summand, (1 - core) * half, half, 1)
        return own, lax.ppermute(other, "rep", core_pairs)

    def over_chips(part):
        if rep_count == 4:
            other = lax.ppermute(part, "rep", [(0, 2), (2, 0), (1, 3), (3, 1)])
            return part.astype(jnp.float32) + other.astype(jnp.float32)
        return lax.psum(part, "rep", axis_index_groups=same_core).astype(jnp.float32)

    def joined(part, core):
        mine = part.astype(jnp.bfloat16)
        other = lax.ppermute(mine, "rep", core_pairs)
        low = jnp.where(core == 0, mine, other)
        high = jnp.where(core == 0, other, mine)
        return jnp.concatenate([low, high], axis=1).astype(jnp.float32)

    def sum_weight(summand, core):
        own, other = sum_owned(summand.astype(jnp.bfloat16), core)
        both = (own.astype(jnp.float32) + other.astype(jnp.float32)).astype(jnp.bfloat16)
        part = lax.psum_scatter(both, "shard", scatter_dimension=0, tiled=True)
        return joined(over_chips(part), core)

    def local(
        tokens,
        cotangent,
        deal_source,
        deal_first,
        deal_length,
        qkv_weight,
        query_bias,
        value_bias,
        out_weight,
        out_bias,
        first_gain,
        first_shift,
        up_weight,
        up_bias,
        down_weight,
        down_bias,
        second_gain,
        second_shift,
    ):
        row_count, width = tokens.shape
        block_count = row_count // BLOCK
        halo = block_count - 1
        pairs = width // PAIR
        shard = lax.axis_index("shard")
        rep = lax.axis_index("rep")
        core = rep % 2
        info = window_info(deal_source[0], deal_first[0], deal_length[0], shard, block_count, halo)
        token_window = with_halo(tokens, halo * BLOCK, shard_count)

        held = qkv_weight.shape[0]
        share = held // rep_count
        hidden_width = up_weight.shape[1]
        grouped = (
            lax.dynamic_slice_in_dim(qkv_weight, rep * share, share, 0)
            .reshape(share, 3, pairs, PAIR)
            .swapaxes(1, 2)
            .reshape(share, 3 * width)
        )
        vectors = (
            query_bias,
            value_bias,
            out_bias,
            first_gain,
            first_shift,
            down_bias,
            second_gain,
            second_shift,
            up_bias,
        )
        lengths = [vector.shape[0] for vector in vectors]
        total = sum(lengths)
        packed = pack_small(vectors, share)
        first_block = jnp.concatenate(
            [grouped, lax.dynamic_slice_in_dim(out_weight, rep * share, share, 0), packed], axis=1
        )
        first_full = lax.all_gather(first_block, ("shard", "rep"), axis=0, tiled=True)
        full_qkv = first_full[:, : 3 * width]
        full_out = first_full[:, 3 * width : 4 * width]
        small = first_full[:, 4 * width :].reshape(shard_count, rep_count, -1)[:, 0, :total]
        small = small.astype(jnp.float32)
        pieces = []
        offset = 0
        for length in lengths:
            pieces.append(small[:, offset : offset + length].reshape(-1))
            offset += length
        (
            bias_query,
            bias_value,
            bias_out,
            gain_one,
            shift_one,
            bias_down,
            gain_two,
            shift_two,
            bias_up,
        ) = pieces
        full_up = lax.all_gather(
            lax.dynamic_slice_in_dim(up_weight, rep * share, share, 0),
            ("shard", "rep"),
            axis=0,
            tiled=True,
        )
        down_share = down_weight.shape[0] // rep_count
        full_down = lax.all_gather(
            lax.dynamic_slice_in_dim(down_weight, rep * down_share, down_share, 0),
            ("shard", "rep"),
            axis=0,
            tiled=True,
        )

        qkv_bias = jnp.stack(
            [
                bias_query.reshape(pairs, PAIR),
                jnp.zeros((pairs, PAIR), jnp.float32),
                bias_value.reshape(pairs, PAIR),
            ],
            axis=1,
        ).reshape(3 * width)
        qkv_window = (matmul(token_window, full_qkv) + qkv_bias).astype(jnp.bfloat16)
        mixed_rows = attend(info, qkv_window, halo, block_count)
        branch = matmul(mixed_rows, full_out) + bias_out
        normed, first_back = jax.vjp(
            layer_norm, tokens.astype(jnp.float32) + branch, gain_one, shift_one
        )
        normed_rows = normed.astype(jnp.bfloat16)

        gate_value = matmul(normed_rows, full_up) + bias_up
        hidden, gelu_back = jax.vjp(gelu_exact, gate_value)
        hidden_rows = hidden.astype(jnp.bfloat16)
        resid_two = normed + matmul(hidden_rows, full_down) + bias_down
        result, second_back = jax.vjp(layer_norm, resid_two, gain_two, shift_two)
        resid_two_grad, second_gain_grad, second_shift_grad = second_back(
            cotangent.astype(jnp.float32)
        )
        second_grad = resid_two_grad.astype(jnp.bfloat16)
        down_bias_grad = jnp.sum(second_grad.astype(jnp.float32), axis=0)
        down_grad = sum_weight(contract_rows(hidden_rows, second_grad), core)
        (gate_grad_full,) = gelu_back(contract_last(second_grad, full_down))
        gate_grad = gate_grad_full.astype(jnp.bfloat16)
        up_bias_grad = jnp.sum(gate_grad.astype(jnp.float32), axis=0)
        up_grad = sum_weight(contract_rows(normed_rows, gate_grad), core)
        normed_grad = resid_two_grad + contract_last(gate_grad, full_up)
        resid_one_grad, first_gain_grad, first_shift_grad = first_back(normed_grad)
        branch_grad = resid_one_grad.astype(jnp.bfloat16)
        out_bias_grad = jnp.sum(branch_grad.astype(jnp.float32), axis=0)
        out_grad = sum_weight(contract_rows(mixed_rows, branch_grad), core)

        mixed_grad = contract_last(branch_grad, full_out).astype(jnp.bfloat16)
        grad_window = with_halo(mixed_grad, halo * BLOCK, shard_count)
        qkv_grad = attend_back(info, qkv_window, grad_window, halo, block_count)
        input_grad = (resid_one_grad + contract_last(qkv_grad, full_qkv)).astype(jnp.bfloat16)
        bias_sums = jnp.sum(qkv_grad.astype(jnp.float32), axis=0).reshape(pairs, 3, PAIR)
        query_bias_grad = bias_sums[:, 0].reshape(width)
        value_bias_grad = bias_sums[:, 2].reshape(width)

        small_grads = (
            query_bias_grad,
            value_bias_grad,
            out_bias_grad,
            first_gain_grad,
            first_shift_grad,
            down_bias_grad,
            second_gain_grad,
            second_shift_grad,
            up_bias_grad,
        )
        flat = jnp.concatenate([piece.reshape(shard_count, -1) for piece in small_grads], axis=1)
        rows_each = -(-total // 128)
        extra = jnp.pad(flat, ((0, 0), (0, rows_each * 128 - total)))
        extra = extra.reshape(shard_count, rows_each, 128)
        extra = jnp.pad(extra, ((0, 0), (0, held - rows_each), (0, 0))).reshape(width, 128)
        extra = extra.astype(jnp.bfloat16)
        own, other = sum_owned(contract_rows(tokens, qkv_grad).astype(jnp.bfloat16), core)
        extra_other = lax.ppermute(extra, "rep", core_pairs)
        both = jnp.concatenate(
            [
                own.astype(jnp.float32) + other.astype(jnp.float32),
                extra.astype(jnp.float32) + extra_other.astype(jnp.float32),
            ],
            axis=1,
        ).astype(jnp.bfloat16)
        part = over_chips(lax.psum_scatter(both, "shard", scatter_dimension=0, tiled=True))
        half = both.shape[1] - 128
        qkv_owned = joined(part[:, :half], core)
        qkv_owned = (
            qkv_owned.reshape(held, pairs, 3, PAIR).swapaxes(1, 2).reshape(held, 3 * width)
        )
        owned_small = part[:rows_each, half:].reshape(-1)
        outs = []
        offset = 0
        for length in lengths:
            outs.append(owned_small[offset : offset + length])
            offset += length
        return (
            result.astype(jnp.bfloat16),
            input_grad,
            qkv_owned,
            outs[0],
            outs[1],
            out_grad,
            outs[2],
            outs[3],
            outs[4],
            up_grad,
            outs[8],
            down_grad,
            outs[5],
            outs[6],
            outs[7],
        )

    return local


def solution(mesh):
    return jax.shard_map(
        make_local(mesh.shape["rep"], mesh.shape["shard"]),
        mesh=mesh,
        in_specs=(
            P(("rep", "shard"), None),
            P(("rep", "shard"), None),
            P("rep", None),
            P("rep", None),
            P("rep", None),
            P("shard", None),
            P("shard"),
            P("shard"),
            P("shard", None),
            P("shard"),
            P("shard"),
            P("shard"),
            P("shard", None),
            P("shard"),
            P("shard", None),
            P("shard"),
            P("shard"),
            P("shard"),
        ),
        out_specs=(
            P(("rep", "shard"), None),
            P(("rep", "shard"), None),
            P("shard", None),
            P("shard"),
            P("shard"),
            P("shard", None),
            P("shard"),
            P("shard"),
            P("shard"),
            P("shard", None),
            P("shard"),
            P("shard", None),
            P("shard"),
            P("shard"),
            P("shard"),
        ),
        check_vma=False,
    )
```

time: 2190 us -> 1030 us (0.47)
  waiting for transfers between devices: 1280 us -> 578 us
  matrix products: 387 us -> 157 us
  blocking collectives: 230 us -> 0 us
  Pallas kernels: 0 us -> 114 us
  local copies, waits for them, and re-layouts: 158 us -> 55.2 us
  other arithmetic: 101 us -> 55 us
  starting transfers between devices: 0.92 us -> 43.8 us
    all_gather x8 -> x3, waiting for transfers between devices: 884 us -> 177 us  [the longest x1 106 us: local(): lax.all_gather(first_block, ('shard', 'rep'), axis=0, tiled=True)]
    dot_general x40 -> x8, matrix products: 334 us -> 105 us  [the longest x4 65.6 us: matmul(): return jnp.dot(left_side, right_side, preferred_element_type=jnp.float32)]
    all_gather x9 -> x0, blocking collectives: 188 us -> none  [the longest x1 27.4 us: mlp_weights(): lax.all_gather(up_bias, 'shard', axis=0, tiled=True)]
    reduce_scatter x4 -> x3, waiting for transfers between devices: 384 us -> 230 us  [sum_weight(): part = lax.psum_scatter(both, 'shard', scatter_dimension=0, tiled=True)]
    pallas_call x0 -> x2, Pallas kernels: none -> 114 us  [the longest x1 80.6 us: attend_back(): pl.pallas_call(functools.partial(backward_kernel, halo=halo, block_count=...]
    ppermute x0 -> x17, waiting for transfers between devices: none -> 94.7 us  [the longest x2 39.2 us: with_halo(): left = lax.ppermute(rows[rows.shape[0] - halo_rows:], 'shard', up)]
    unnamed x13 -> x8, waiting for transfers between devices: 4.43 us -> 75.3 us
    reshape x2 -> x5, local copies, waits for them, and re-layouts: 52 us -> 1.5 us  [the longest x1 0.85 us: local(): grouped = lax.dynamic_slice_in_dim(qkv_weight, rep * share, share, 0).res...]
  transfers between devices with their start and end apart: 13 -> 24, of which waited for: 11 -> 14; matrix products, arithmetic and copies ran while one was open for 23% -> 17% of each run, Pallas kernels for 0% -> 11%
where the time goes in v1:
time: 1030 us; the launch traced here: 1020 us
  waiting for transfers between devices  578 us (56%)
  matrix products  157 us (15%)
  Pallas kernels  114 us (11%)
  local copies, waits for them, and re-layouts  55.2 us (5%)
  other arithmetic  55 us (5%)
  starting transfers between devices  43.8 us (4%)
  between operations  16.3 us (2%)
    reduce_scatter x3, waiting for transfers between devices, sum_weight(): part = lax.psum_scatter(both, 'shard', scatter_dimension=0, tiled=True)  230 us
    all_gather x1, waiting for transfers between devices, local(): lax.all_gather(first_block, ('shard', 'rep'), axis=0, tiled=True)  106 us
    pallas_call x1, Pallas kernels, attend_back(): pl.pallas_call(functools.partial(backward_kernel, halo=halo, block_count=...  80.6 us
    unnamed x8, waiting for transfers between devices  75.3 us
    dot_general x4, matrix products, matmul(): return jnp.dot(left_side, right_side, preferred_element_type=jnp.float32)  65.6 us
    all_gather x1, waiting for transfers between devices, local(): lax.all_gather(lax.dynamic_slice_in_dim(down_weight, rep * down_share, do...  58.2 us
    dot_general x4, matrix products, contract_last(): lax.dot_general(left_side, right_side, (((1,), (1,)), ((), ())), preferre...  52 us
    dot_general x4, matrix products, contract_rows(): lax.dot_general(left_side, right_side, (((0,), (0,)), ((), ())), preferre...  39.3 us
  transfers between devices with their start and end apart: 24, of which 14 were waited for; matrix products, arithmetic and copies ran while one was open for 17% of the time, Pallas kernels for 11%

profile of v1, /device:TPU:0, one launch (start us, length us, event | category | flops | bytes accessed | tf_op | source)
XLA Modules:
  0.0 1018.3 jit_solution(12741556865428770672)
XLA Ops:
  42.5 106.3 %all-gather.4.cloned.1.call-done = bf16[1024,4224]{1,0:T(8,128)(2,1)} async-done(((bf16[32,4224]{1,0:T(8,128)(2,1)}), bf16[1024,4224]{1,0:T(8,128)(2,1)}) %all-gather.4.cloned.1.call-update) | async-done | bytes 8650768 | tf_op jit(solution)/shard_map/all_gather | solution.py:301
  150.1 23.8 %add_convert_fusion.qkv = bf16[2816,3072]{1,0:T(8,128)(2,1)} fusion(f32[3072]{0:T(1024)S(1)} %add.205, bf16[896,1024]{1,0:T(8,128)(2,1)} %collective-permute-done.1, bf16[1024,1024]{1,0:T(8,128)(2,1)S(1)} %copy-done.4, bf16[896,1024]{1,0:T(8,128)(2,1)} %collective-permute-done, bf16[1024,4224]{1,0:T(8,128)(2,1)} %all-gather.4.cloned.1.call-done), kind=kOutput, calls=%fused_computation | convolution fusion | flops 17751343104 | bytes 29372416 | tf_op jit(solution)/shard_map/dot_general | solution.py:41
  173.9 32.9 %attend.1 = bf16[1024,1024]{1,0:T(8,128)(2,1)} custom-call(s32[3,22]{1,0:T(4,128)} %pad_add_fusion.info, bf16[2816,3072]{1,0:T(8,128)(2,1)} %add_convert_fusion.qkv), custom_call_target="tpu_custom_call" | custom-call | tf_op jit(solution)/shard_map/attend/pallas_call | solution.py:144
  216.3 12.5 %all-gather.6.cloned.1.call-done = bf16[1024,4096]{1,0:T(8,128)(2,1)} async-done(((bf16[32,4096]{1,0:T(8,128)(2,1)}), bf16[1024,4096]{1,0:T(8,128)(2,1)}) %all-gather.6.cloned.1.call-update) | async-done | bytes 8388624 | tf_op jit(solution)/shard_map/all_gather | solution.py:322
  228.8 20.1 %multiply_convert_fusion = (bf16[1024,4096]{1,0:T(8,128)(2,1)}, f32[1024,4096]{1,0:T(8,128)}) fusion(f32[4096]{0:T(1024)S(1)} %bitcast.111, bf16[1024,4096]{1,0:T(8,128)(2,1)} %all-gather.6.cloned.1.call-done, f32[1024,1024]{0,1:T(8,128)} %get-tuple-element.143, f32[1024]{0:T(1024)S(1)} %get-tuple-element.133, f32[1024]{0:T(1024)S(1)} %get-tuple-element.134, ...), kind=kOutput, calls=%fused_computation.2 | convolution fusion | flops 8620343296 | bytes 37781504 | tf_op jit(solution)/shard_map/dot_general | solution.py:41
  248.9 58.2 %all-gather.8.cloned.1.call-done = bf16[4096,1024]{1,0:T(8,128)(2,1)} async-done(((bf16[128,1024]{1,0:T(8,128)(2,1)}), bf16[4096,1024]{1,0:T(8,128)(2,1)}) %all-gather.8.cloned.1.call-update) | async-done | bytes 8388624 | tf_op jit(solution)/shard_map/all_gather | solution.py:329
  307.1 14.9 %fusion.39 = (f32[1024]{0:T(1024)S(1)}, f32[1024,1024]{0,1:T(8,128)S(1)}) fusion(f32[1024]{0:T(1024)S(1)} %get-tuple-element.132, bf16[1024,4096]{1,0:T(8,128)(2,1)} %get-tuple-element.144, bf16[4096,1024]{1,0:T(8,128)(2,1)} %all-gather.8.cloned.1.call-done, f32[1024]{0:T(1024)S(1)} %get-tuple-element.133, f32[1024]{0:T(1024)S(1)} %get-tuple-element.134, ...), kind=kOutput, calls=%fused_computation.148 | convolution fusion | flops 8597273600 | bytes 25190400 | tf_op jit(solution)/shard_map/dot_general | solution.py:41
  331.2 20.0 %fusion.31 = (bf16[4096]{0:T(1024)(128)(2,1)S(1)}, bf16[1024,4096]{1,0:T(8,128)(2,1)}) fusion(f32[1024,4096]{1,0:T(8,128)} %get-tuple-element.145, f32[4096]{0:T(1024)S(1)} %bitcast.112, bf16[1024,1024]{0,1:T(8,128)(2,1)S(1)} %get-tuple-element.110, bf16[4096,1024]{1,0:T(8,128)(2,1)S(1)} %bitcast.120), kind=kOutput, calls=%fused_computation.140 | convolution fusion | flops 8652845056 | bytes 35676160 | tf_op jit(solution)/shard_map/dot_general | solution.py:29
  351.1 16.7 %multiply_reduce_fusion = (bf16[1024]{0:T(1024)(128)(2,1)S(1)}, f32[1024]{0:T(1024)S(1)}, bf16[1024]{0:T(1024)(128)(2,1)S(1)}, f32[1024,1024]{0,1:T(8,128)S(1)}) fusion(f32[1024,1024]{0,1:T(8,128)} %get-tuple-element.143, f32[1024]{0:T(1024)S(1)} %fusion.21, f32[1024]{0:T(1024)S(1)} %broadcast_multiply_fusion.1, f32[1024]{0:T(1024)S(1)} %get-tuple-element.134, ...), kind=kOutput, calls=%fused_computation.28 | convolution fusion | flops 8607757312 | bytes 31498240 | tf_op jit(solution)/shard_map/dot_general | solution.py:29
  392.7 31.2 %collective-permute-done.3 = bf16[896,1024]{1,0:T(8,128)(2,1)} collective-permute-done((bf16[896,1024]{1,0:T(8,128)(2,1)}, bf16[896,1024]{1,0:T(8,128)(2,1)}, u32[]{:S(2)}, u32[]{:S(2)}) %collective-permute-start.3) | collective-permute-done | bytes 1835040 | tf_op jit(solution)/shard_map/ppermute | solution.py:206
  423.9 39.2 %collective-permute-done.2 = bf16[896,1024]{1,0:T(8,128)(2,1)} collective-permute-done((bf16[896,1024]{1,0:T(8,128)(2,1)}, bf16[896,1024]{1,0:T(8,128)(2,1)}, u32[]{:S(2)}, u32[]{:S(2)}) %collective-permute-start.2) | collective-permute-done | bytes 1835040 | tf_op jit(solution)/shard_map/ppermute | solution.py:205
  468.3 80.6 %attend_back.1 = bf16[1024,3072]{1,0:T(8,128)(2,1)} custom-call(s32[3,22]{1,0:T(4,128)} %pad_add_fusion.info, bf16[2816,3072]{1,0:T(8,128)(2,1)} %add_convert_fusion.qkv, bf16[2816,1024]{1,0:T(8,128)(2,1)} %pad_maximum_fusion.mixed_grad), custom_call_target="tpu_custom_call" | custom-call | tf_op jit(solution)/shard_map/attend_back/pallas_call | solution.py:161
  548.9 9.8 convolution_convert_fusion.2
  563.2 20.9 %collective-permute-start.4 = (bf16[1024,1536]{0,1:T(8,128)(2,1)}, bf16[1024,1536]{0,1:T(8,128)(2,1)}, u32[]{:S(2)}, u32[]{:S(2)}) collective-permute-start(bf16[1024,1536]{0,1:T(8,128)(2,1)} %dynamic-slice_bitcast_fusion), channel_id=1, source_target_pairs={{0,8},{8,0},{16,24},{24,16},{1,9},{9,1},{17,25},{25,17},{2,10},{10... | collective-permute-start | bytes 9437192 | tf_op jit(solution)/shard_map/ppermute | solution.py:224
  601.7 13.6 %convolution_convert_fusion.1 = bf16[1024,4096]{1,0:T(8,128)(2,1)S(1)} fusion(bf16[1024,4096]{1,0:T(8,128)(2,1)} %get-tuple-element.108, f32[1024,1024]{0,1:T(8,128)} %get-tuple-element.143, f32[1024]{0:T(1024)S(1)} %get-tuple-element.133, f32[1024]{0:T(1024)S(1)} %get-tuple-element.134, f32[1024]{0:T(1024)S(1)} %fusion.21, ...), kind=kOutput, calls=%fused_computation.7 | convolution fusion | flops 8599371776 | bytes 20987904 | tf_op jit(solution)/shard_map/dot_general | solution.py:35
  620.1 7.2 collective-permute-done.11
  627.3 7.8 add_convert_fusion.3
  636.7 11.4 %convolution_convert_fusion = bf16[4096,1024]{1,0:T(8,128)(2,1)S(1)} fusion(bf16[1024,4096]{1,0:T(8,128)(2,1)} %get-tuple-element.144, bf16[1024,1024]{0,1:T(8,128)(2,1)S(1)} %copy-done.14), kind=kOutput, calls=%fused_computation.6 | convolution fusion | flops 8594128896 | bytes 18874368 | tf_op jit(solution)/shard_map/dot_general | solution.py:35
  659.7 68.7 %reduce-scatter.7.cloned.1.call-done = bf16[128,512]{1,0:T(8,128)(2,1)} async-done(((bf16[1024,512]{1,0:T(8,128)(2,1)}), bf16[128,512]{1,0:T(8,128)(2,1)}) %reduce-scatter.7.cloned.1.call-update) | async-done | bytes 131088 | tf_op jit(solution)/shard_map/reduce_scatter | solution.py:242
  733.7 75.2 %reduce-scatter.13.cloned.1.call-done = bf16[128,1664]{1,0:T(8,128)(2,1)} async-done(((bf16[1024,1664]{1,0:T(8,128)(2,1)}), bf16[128,1664]{1,0:T(8,128)(2,1)}) %reduce-scatter.13.cloned.1.call-update) | async-done | bytes 426000
  811.8 11.3 %add_convert_fusion.4 = bf16[1024,1024]{0,1:T(8,128)(2,1)S(1)} fusion(f32[1024,1024]{0,1:T(8,128)} %copy-done.3, f32[1024]{0:T(1024)S(1)} %negate_multiply_fusion, bf16[1024,3072]{1,0:T(8,128)(2,1)} %attend_back.1, bf16[1024,4224]{1,0:T(8,128)(2,1)} %all-gather.4.cloned.1.call-done), kind=kOutput, calls=%fused_computation.29 | convolution fusion | flops 6445596672 | bytes 18878464 | tf_op jit(solution)/shard_map/dot_general | solution.py:29
  826.7 73.3 %reduce-scatter.9.cloned.1.call-done = bf16[128,2048]{1,0:T(8,128)(2,1)} async-done(((bf16[1024,2048]{1,0:T(8,128)(2,1)}), bf16[128,2048]{1,0:T(8,128)(2,1)}) %reduce-scatter.9.cloned.1.call-update) | async-done | bytes 524304 | tf_op jit(solution)/shard_map/reduce_scatter | solution.py:242
  903.3 88.4 %reduce-scatter.11.cloned.1.call-done = bf16[512,512]{1,0:T(8,128)(2,1)} async-done(((bf16[4096,512]{1,0:T(8,128)(2,1)}), bf16[512,512]{1,0:T(8,128)(2,1)}) %reduce-scatter.11.cloned.1.call-update) | async-done | bytes 524304 | tf_op jit(solution)/shard_map/reduce_scatter | solution.py:242
  997.4 8.0 collective-permute-done.15
  (193 shorter events, 150.0 us)
Async XLA Ops:
  7.2 141.6 %all-gather.4.cloned.1.call-start = ((), (), s32[]{:S(2)}) async-start(), calls=%async_computation.4 | async-start | bytes 8921088 | tf_op jit(solution)/shard_map/all_gather | solution.py:301
  19.3 209.5 %all-gather.6.cloned.1.call-start = ((), (), s32[]{:S(2)}) async-start(), calls=%async_computation.5 | async-start | bytes 8650752 | tf_op jit(solution)/shard_map/all_gather | solution.py:322
  20.1 287.1 %all-gather.8.cloned.1.call-start = ((), (), s32[]{:S(2)}) async-start(), calls=%async_computation.6 | async-start | bytes 8650752 | tf_op jit(solution)/shard_map/all_gather | solution.py:329
  21.8 706.6 %reduce-scatter.7.cloned.1.call-start = ((), (), s32[]{:S(2)}) async-start(), calls=%async_computation.7 | async-start | bytes 1179648 | tf_op jit(solution)/shard_map/reduce_scatter | solution.py:242
  24.2 125.8 %collective-permute-start.1 = (bf16[896,1024]{1,0:T(8,128)(2,1)}, bf16[896,1024]{1,0:T(8,128)(2,1)}, u32[]{:S(2)}, u32[]{:S(2)}) collective-permute-start(bf16[896,1024]{1,0:T(8,128)(2,1)} %get-tuple-element.121), channel_id=1, source_target_pairs={{1,0},{2,1},{3,2},{4,3},{5,4},{6,5},{7,6},{9,8},{10,9},{11,10},{12... | collective-permute-start | bytes 5505032 | tf_op jit(solution)/shard_map/ppermute | solution.py:206
  25.5 124.5 %collective-permute-start = (bf16[896,1024]{1,0:T(8,128)(2,1)}, bf16[896,1024]{1,0:T(8,128)(2,1)}, u32[]{:S(2)}, u32[]{:S(2)}) collective-permute-start(bf16[896,1024]{1,0:T(8,128)(2,1)} %get-tuple-element.120), channel_id=1, source_target_pairs={{0,1},{1,2},{2,3},{3,4},{4,5},{5,6},{6,7},{8,9},{9,10},{10,11},{11... | collective-permute-start | bytes 5505032 | tf_op jit(solution)/shard_map/ppermute | solution.py:205
  379.6 44.4 %collective-permute-start.3 = (bf16[896,1024]{1,0:T(8,128)(2,1)}, bf16[896,1024]{1,0:T(8,128)(2,1)}, u32[]{:S(2)}, u32[]{:S(2)}) collective-permute-start(bf16[896,1024]{1,0:T(8,128)(2,1)} %get-tuple-element.119), channel_id=1, source_target_pairs={{1,0},{2,1},{3,2},{4,3},{5,4},{6,5},{7,6},{9,8},{10,9},{11,10},{12... | collective-permute-start | bytes 5505032 | tf_op jit(solution)/shard_map/ppermute | solution.py:206
  380.9 82.3 %collective-permute-start.2 = (bf16[896,1024]{1,0:T(8,128)(2,1)}, bf16[896,1024]{1,0:T(8,128)(2,1)}, u32[]{:S(2)}, u32[]{:S(2)}) collective-permute-start(bf16[896,1024]{1,0:T(8,128)(2,1)} %get-tuple-element.118), channel_id=1, source_target_pairs={{0,1},{1,2},{2,3},{3,4},{4,5},{5,6},{6,7},{8,9},{9,10},{10,11},{11... | collective-permute-start | bytes 5505032 | tf_op jit(solution)/shard_map/ppermute | solution.py:205
  392.7 191.8 %collective-permute-start.8 = (bf16[1024,512]{1,0:T(8,128)(2,1)S(1)}, bf16[1024,512]{1,0:T(8,128)(2,1)}, u32[]{:S(2)}, u32[]{:S(2)}) collective-permute-start(bf16[1024,512]{1,0:T(8,128)(2,1)S(1)} %constant_dynamic-slice_fusion.2), channel_id=1, source_target_pairs={{0,8},{8,0},{16,24},{24,16},{1,9},{9,1},{17,25},{25,17},{2,10},{10... | collective-permute-start | bytes 3145736 | tf_op jit(solution)/shard_map/ppermute | solution.py:224
  563.2 30.0 %collective-permute-start.4 = (bf16[1024,1536]{0,1:T(8,128)(2,1)}, bf16[1024,1536]{0,1:T(8,128)(2,1)}, u32[]{:S(2)}, u32[]{:S(2)}) collective-permute-start(bf16[1024,1536]{0,1:T(8,128)(2,1)} %dynamic-slice_bitcast_fusion), channel_id=1, source_target_pairs={{0,8},{8,0},{16,24},{24,16},{1,9},{9,1},{17,25},{25,17},{2,10},{10... | collective-permute-start | bytes 9437192 | tf_op jit(solution)/shard_map/ppermute | solution.py:224
  587.3 221.6 %reduce-scatter.13.cloned.1.call-start = ((), (), s32[]{:S(2)}) async-start(), calls=%async_computation.10 | async-start | bytes 3833856
  591.6 1.6 collective-permute-start.5
  601.7 298.4 %reduce-scatter.9.cloned.1.call-start = ((), (), s32[]{:S(2)}) async-start(), calls=%async_computation.8 | async-start | bytes 4718592 | tf_op jit(solution)/shard_map/reduce_scatter | solution.py:242
  619.8 7.5 collective-permute-start.11
  635.1 356.6 %reduce-scatter.11.cloned.1.call-start = ((), (), s32[]{:S(2)}) async-start(), calls=%async_computation.9 | async-start | bytes 4718592 | tf_op jit(solution)/shard_map/reduce_scatter | solution.py:242
  648.6 7.2 collective-permute-start.14
  728.4 5.2 collective-permute-start.9
  733.7 92.2 %collective-permute-start.10 = (bf16[128,512]{1,0:T(8,128)(2,1)S(1)}, bf16[128,512]{1,0:T(8,128)(2,1)S(1)}, u32[]{:S(2)}, u32[]{:S(2)}) collective-permute-start(bf16[128,512]{1,0:T(8,128)(2,1)S(1)} %add_convert_fusion.12), channel_id=1, source_target_pairs={{0,8},{8,0},{16,24},{24,16},{1,9},{9,1},{17,25},{25,17},{2,10},{10... | collective-permute-start | bytes 393224 | tf_op jit(solution)/shard_map/ppermute | solution.py:234
  810.2 91.3 %collective-permute-start.6 = (bf16[128,1664]{0,1:T(8,128)(2,1)S(1)}, bf16[128,1664]{0,1:T(8,128)(2,1)S(1)}, u32[]{:S(2)}, u32[]{:S(2)}) collective-permute-start(bf16[128,1664]{0,1:T(8,128)(2,1)S(1)} %copy.90), channel_id=1, source_target_pairs={{0,16},{16,0},{8,24},{24,8},{1,17},{17,1},{9,25},{25,9},{2,18},{18... | collective-permute-start | bytes 1277960 | tf_op jit(solution)/shard_map/ppermute | solution.py:228
  900.0 93.2 %collective-permute-start.12 = (bf16[128,2048]{1,0:T(8,128)(2,1)}, bf16[128,2048]{1,0:T(8,128)(2,1)S(1)}, u32[]{:S(2)}, u32[]{:S(2)}) collective-permute-start(bf16[128,2048]{1,0:T(8,128)(2,1)} %reduce-scatter.9.cloned.1.call-done), channel_id=1, source_target_pairs={{0,16},{16,0},{8,24},{24,8},{1,17},{17,1},{9,25},{25,9},{2,18},{18... | collective-permute-start | bytes 1572872 | tf_op jit(solution)/shard_map/ppermute | solution.py:228
  901.7 93.4 %collective-permute-start.7 = (bf16[128,1536]{0,1:T(8,128)(2,1)S(1)}, bf16[128,1536]{0,1:T(8,128)(2,1)S(1)}, u32[]{:S(2)}, u32[]{:S(2)}) collective-permute-start(bf16[128,1536]{0,1:T(8,128)(2,1)S(1)} %slice.226), channel_id=1, source_target_pairs={{0,8},{8,0},{16,24},{24,16},{1,9},{9,1},{17,25},{25,17},{2,10},{10... | collective-permute-start | bytes 1179656 | tf_op jit(solution)/shard_map/ppermute | solution.py:234
  991.7 13.6 %collective-permute-start.15 = (bf16[512,512]{1,0:T(8,128)(2,1)}, bf16[512,512]{1,0:T(8,128)(2,1)}, u32[]{:S(2)}, u32[]{:S(2)}) collective-permute-start(bf16[512,512]{1,0:T(8,128)(2,1)} %reduce-scatter.11.cloned.1.call-done), channel_id=1, source_target_pairs={{0,16},{16,0},{8,24},{24,8},{1,17},{17,1},{9,25},{25,9},{2,18},{18... | collective-permute-start | bytes 1572872 | tf_op jit(solution)/shard_map/ppermute | solution.py:228
  995.2 11.6 %collective-permute-start.13 = (bf16[128,2048]{1,0:T(8,128)(2,1)}, bf16[128,2048]{1,0:T(8,128)(2,1)}, u32[]{:S(2)}, u32[]{:S(2)}) collective-permute-start(bf16[128,2048]{1,0:T(8,128)(2,1)} %add_convert_fusion.10), channel_id=1, source_target_pairs={{0,8},{8,0},{16,24},{24,16},{1,9},{9,1},{17,25},{25,17},{2,10},{10... | collective-permute-start | bytes 1572872 | tf_op jit(solution)/shard_map/ppermute | solution.py:234
  1006.7 2.9 collective-permute-start.16
  (21 other events, 318.8 us)
Sparse Core Ops, SparseCore 0:
  19.4 129.3 all-gather.3
  152.3 76.4 all-gather.5
  231.7 75.4 all-gather.7
  587.5 140.9 reduce-scatter.6
  731.9 77.0 reduce-scatter.12
  812.4 87.5 reduce-scatter.8
  903.7 88.0 reduce-scatter.10
